TPU v7x, 32 devices: a whole 2x2x4 slice. The times are simulated.
32 devices in a mesh: groups: 2 (over x), branch: 16 (over z, y, core).
Axes of the slice: x: 2, y: 2, z: 4, core: 2. Of those that a mesh axis runs over, the one named last changes fastest.
Arguments:
- prompt_k: bfloat16 [32, 1024, 1024], P(('groups', 'branch')), parts along dimension 0, may hold values from -6 to 6
- prompt_v: bfloat16 [32, 1024, 1024], P(('groups', 'branch')), parts along dimension 0, may hold values from -6 to 6
- prompt_mask: int32 [32, 8], P(('groups', 'branch')), parts along dimension 0, may hold values from 0 to 1, as said below
- shared_kv: bfloat16 [64, 24, 2048], P(('groups', 'branch')), parts along dimension 0, may hold values from -6 to 6
- shared_len: int32 [64], P(('groups', 'branch')), parts along dimension 0, may hold values from 1 to 24, 400 in all
- send_pick: int32 [32, 16], P(('groups', 'branch')), parts along dimension 0, may hold values from -1 to 1, as said below
- unique_q: bfloat16 [512, 8192], P(('groups', 'branch')), parts along dimension 0, may hold values from -132 to 132
- unique_kv: bfloat16 [512, 2048], P(('groups', 'branch')), parts along dimension 0, may hold values from -6.5 to 6.5
- unique_owner: int32 [512, 1], P(('groups', 'branch')), parts along dimension 0, may hold values from 0 to 15; in each aligned block of 16 rows (0 to 15, 16 to 31, ...) at most 2 rows name the same one
Outputs:
- attended: bfloat16 [512, 8192], P(('groups', 'branch')), parts along dimension 0
There are 2 independent parts, one for each index of `groups`. A program takes and returns all parts, laid end to end along the dimension named above; each array names one. Nothing has to cross between parts.
Inputs may be any that keep to these rules, and one draw needn't show every extreme that they name: `prompt_mask`: block 0 of every branch's prompt is visible. `send_pick`: entry [s, b] names which of owner s's 2 results branch b subscribes to, or -1 for none; every branch subscribes to exactly 12 results, at most one of each owner. `unique_owner`: among the rows of one source, no branch is named by more than 2 rows.
All inputs are finite; a program needn't handle non-finite values. No bound on the sum of `shared_len` on one device may be relied on, other than what follows from the above.
Results may differ from a plain program's by a relative error of at most 0.0027.
Values may be sent and summed in bfloat16 or wider, within the bound.
A program may use at most 128 MiB of HBM per device.

v0:
```python
import functools
import math

import jax
import jax.numpy as jnp
from jax import lax
from jax.experimental import pallas as pl
from jax.experimental.pallas import tpu as pltpu
from jax.sharding import PartitionSpec as P

HD = 128
GRP = 8
NEG = -1e30
MESH = pl.DeviceIdType.MESH


def kernel(
    n, across, cap, rlen, res, heads,
    owner_ref, pick_ref, len_ref, mask_ref, q_ref, kv_ref, shared_ref, pk_hbm, pv_hbm,
    out_ref,
    pk, pv, flat, by_row, slot_of, pbias, meta_ref, xs, xr, mr, gath, tail, kslot, acc, stat, ox, orx,
    psem, lsem, xsend, xrecv, msend, mrecv, gsend, grecv, rsend, rrecv,
):
    me = lax.axis_index("branch")
    kvh = heads // GRP
    pairs = kvh // 2
    width = n * cap
    rows = width * GRP
    kvw = kvh * HD
    line = n // (2 * across)
    core = lax.rem(me, 2)
    chip = me // 2
    y = lax.rem(chip, across)
    z = chip // across
    sibling = me + 1 - 2 * core
    tail_n = tail.shape[0]
    scale = math.log2(math.e) / math.sqrt(HD)

    copy_k = pltpu.make_async_copy(pk_hbm.at[0], pk, psem.at[0])
    copy_v = pltpu.make_async_copy(pv_hbm.at[0], pv, psem.at[1])
    copy_k.start()
    copy_v.start()

    barrier = pltpu.get_barrier_semaphore()

    def greet(i, c):
        pl.semaphore_signal(
            barrier, inc=1, device_id={"branch": lax.rem(me + i, n)}, device_id_type=MESH
        )
        return c

    lax.fori_loop(1, n, greet, 0)

    count = q_ref.shape[0]
    per = heads + 2 * kvh
    some = min(count, 16)
    for r in range(0, count, some):
        for h in range(per):
            ref, g = (q_ref, h) if h < heads else (kv_ref, h - heads)
            flat[pl.ds(h, some, stride=per), :] = ref[
                r : r + some, g * HD : (g + 1) * HD
            ].astype(jnp.float32)
        for i in range(some):
            by_row[r + i] = flat[i * per : (i + 1) * per].astype(jnp.bfloat16)

    def number(j, c):
        mine = owner_ref[j]
        rank = lax.fori_loop(
            0, j, lambda i, r: r + jnp.where(owner_ref[i] == mine, 1, 0), jnp.int32(0)
        )
        slot_of[j] = mine * cap + rank
        return c

    lax.fori_loop(0, count, number, 0)

    def place(b, c):
        def scan(r, found):
            for u in range(some):
                i = r * some + u
                hit = owner_ref[i] == b
                rows_at, seen = found[:cap], found[cap]
                rows_at = [
                    jnp.where(jnp.logical_and(hit, seen == k), i, at)
                    for k, at in enumerate(rows_at)
                ]
                found = (*rows_at, seen + jnp.where(hit, 1, 0))
            return found

        found = lax.fori_loop(0, count // some, scan, (jnp.int32(0),) * (cap + 1))
        pick = pick_ref[0, b]
        length = jnp.int32(0)
        for e in range(res):
            length = jnp.where(pick == e, len_ref[e], length)
        meta_ref[b, 0:1] = jnp.full((1, HD), pick, jnp.int32)
        meta_ref[b, 1:2] = jnp.full((1, HD), length, jnp.int32)
        for k in range(cap):
            xs[b * cap + k] = by_row[found[k]]
            meta_ref[b, 2 + k : 3 + k] = jnp.full(
                (1, HD), jnp.where(found[cap] > k, 1, 0), jnp.int32
            )
        return c

    lax.fori_loop(0, n, place, 0)
    blocks = mask_ref.shape[1]
    block = pk.shape[0] // blocks
    for g in range(blocks):
        pbias[:, g * block : (g + 1) * block] = jnp.full(
            (1, block), jnp.where(mask_ref[0, g] > 0, 0.0, NEG), jnp.float32
        )
    pl.semaphore_wait(barrier, n - 1)

    def ship(src, source, e, target, way):
        return pltpu.make_async_remote_copy(
            src_ref=src,
            dst_ref=gath.at[source, e],
            send_sem=gsend.at[way, source * res + e],
            recv_sem=grecv.at[source * res + e],
            device_id={"branch": target},
            device_id_type=MESH,
        )

    def member(zz, yy, cc):
        return (zz * across + yy) * 2 + cc

    def spread(zs, e, first, act):
        source = member(zs, y, core)
        src = shared_ref.at[e] if first else gath.at[source, e]

        @pl.when(jnp.logical_and(zs <= z, z + 1 < line))
        def _():
            act(ship(src, source, e, member(lax.rem(z + 1, line), y, core), 0))

        @pl.when(jnp.logical_and(zs >= z, z >= 1))
        def _():
            act(ship(src, source, e, member(lax.rem(z + line - 1, line), y, core), 1))

        for d in range(1, across):
            act(ship(src, source, e, member(z, lax.rem(y + d, across), core), 1 + d))
        act(ship(src, source, e, sibling, 1 + across))

    def arrived(source, e):
        ship(gath.at[source, e], source, e, sibling, 0).wait_recv()

    begin = lambda copy: copy.start()
    finish = lambda copy: copy.wait_send()

    def on_line(t, act, waits):
        for up in (0, 1):
            zs = z - t if up == 0 else z + t
            ok = zs >= 0 if up == 0 else zs < line

            @pl.when(ok)
            def _():
                zc = lax.rem(zs + line, line)
                for e in range(res):
                    if waits:
                        arrived(member(zc, y, core), e)
                    spread(zc, e, False, act)

    def cross(zs, act, waits):
        for d in range(1, across):
            source = member(zs, lax.rem(y + d, across), core)
            for e in range(res):
                if waits:
                    arrived(source, e)
                act(ship(gath.at[source, e], source, e, sibling, 1 + across))

    def off_line(t, act, waits):
        @pl.when(z - t >= 0)
        def _():
            cross(lax.rem(z - t + line, line), act, waits)

        @pl.when(jnp.logical_and(z + t < line, t > 0))
        def _():
            cross(lax.rem(z + t, line), act, waits)

    def relay(t, c):
        on_line(t, begin, True)
        off_line(t - 1, begin, True)
        return c


    def part(ref, b):
        return ref.at[pl.ds(b * cap, cap)]

    def x_copy(i, b, at):
        return pltpu.make_async_remote_copy(
            src_ref=part(xs, b), dst_ref=part(xr, at), send_sem=xsend.at[i], recv_sem=xrecv.at[i],
            device_id={"branch": b}, device_id_type=MESH,
        )

    def m_copy(i, b, at):
        return pltpu.make_async_remote_copy(
            src_ref=meta_ref.at[b], dst_ref=mr.at[at], send_sem=msend.at[i], recv_sem=mrecv.at[i],
            device_id={"branch": b}, device_id_type=MESH,
        )

    def send_x(i, c):
        b = lax.rem(me + i, n)
        x_copy(i, b, me).start()
        m_copy(i, b, me).start()
        return c

    lax.fori_loop(1, n, send_x, 0)
    for e in range(res):
        spread(z, e, True, begin)
    own_x = pltpu.make_async_copy(part(xs, me), part(xr, me), lsem.at[0])
    own_m = pltpu.make_async_copy(meta_ref.at[me], mr.at[me], lsem.at[1])
    own_x.start()
    own_m.start()
    gath[me] = shared_ref[...]
    tail[...] = jnp.zeros_like(tail)

    def take_x(i, c):
        b = lax.rem(me + n - i, n)
        x_copy(i, b, b).wait_recv()
        m_copy(i, b, b).wait_recv()
        return c

    lax.fori_loop(1, n, take_x, 0)
    own_x.wait()
    own_m.wait()
    copy_k.wait()
    copy_v.wait()

    def queries(p):
        both = xr[:, pl.ds(p * 2 * GRP, 2 * GRP), :].astype(jnp.float32)
        return [
            both[:, k * GRP : (k + 1) * GRP].reshape(rows, HD).astype(jnp.bfloat16)
            for k in range(2)
        ]

    def scores(q, k):
        return lax.dot_general(q, k, (((1,), (1,)), ((), ())), preferred_element_type=jnp.float32)

    half = lax.broadcasted_iota(jnp.int32, (rows, HD), 1) < HD // 2

    def prompt_pair(p):
        for k, q in enumerate(queries(p)):
            h = 2 * p + k
            cols = slice(h * HD, (h + 1) * HD)
            s = scores(q, pk[:, cols]) * scale + pbias[...]
            m = jnp.max(s, axis=-1, keepdims=True)
            w = jnp.exp2(s - m)
            stat[h] = jnp.where(half, m, jnp.sum(w, axis=-1, keepdims=True))
            acc[h] = jnp.dot(
                w.astype(jnp.bfloat16), pv[:, cols], preferred_element_type=jnp.float32
            )

    cuts = [1 + (line - 1) * p // pairs for p in range(pairs + 1)]
    for p in range(pairs):
        prompt_pair(p)
        if cuts[p] < cuts[p + 1]:
            lax.fori_loop(cuts[p], cuts[p + 1], relay, 0)
    off_line(line - 1, begin, True)

    flat[: width * 2 * kvh] = (
        xr[:, heads:, :].astype(jnp.float32).reshape(width * 2 * kvh, HD)
    )
    for j in range(2 * kvh):
        tail[n * rlen : n * rlen + width, j * HD : (j + 1) * HD] = flat[
            pl.ds(j, width, stride=2 * kvh), :
        ].astype(jnp.bfloat16)
    col = lax.broadcasted_iota(jnp.int32, (1, tail_n), 1)

    def limits(s, carry):
        length, live = carry
        meta = mr[s]
        length = jnp.where(col // rlen == s, meta[1:2, 0:1], length)
        for k in range(cap):
            live = jnp.where(col == n * rlen + s * cap + k, meta[2 + k : 3 + k, 0:1], live)
        return length, live

    zero = jnp.zeros((1, tail_n), jnp.int32)
    length, live = lax.fori_loop(0, n, limits, (zero, zero))
    shared_ok = jnp.logical_and(col < n * rlen, lax.rem(col, rlen) < length)
    kslot[...] = jnp.where(shared_ok, -1, jnp.where(live > 0, col - n * rlen, width))
    row_slot = lax.broadcasted_iota(jnp.int32, (rows, 1), 0) // GRP

    def far(i, c):
        for yy in range(across):
            source = member(i, yy, 1 - core)
            for e in range(res):
                arrived(source, e)
        return c

    lax.fori_loop(0, line, far, 0)

    def choose(t, c):
        two = []
        for s in (2 * t, 2 * t + 1):
            pick = mr[s][0:1, 0:1]
            chosen = gath[s, 0].astype(jnp.float32)
            for e in range(1, res):
                chosen = jnp.where(pick == e, gath[s, e].astype(jnp.float32), chosen)
            two.append(chosen)
        tail[pl.ds(pl.multiple_of(t * 2 * rlen, 16), 2 * rlen), :] = jnp.concatenate(
            two, axis=0
        ).astype(jnp.bfloat16)
        return c

    lax.fori_loop(0, n // 2, choose, 0)

    def tail_pair(p):
        done = []
        for k, q in enumerate(queries(p)):
            h = 2 * p + k
            keys = tail[:, h * HD : (h + 1) * HD]
            values = tail[:, kvw + h * HD : kvw + (h + 1) * HD]
            s = jnp.where(kslot[...] <= row_slot, scores(q, keys) * scale, NEG)
            before = stat[h][:, :1]
            m = jnp.maximum(before, jnp.max(s, axis=-1, keepdims=True))
            w = jnp.exp2(s - m)
            keep = jnp.exp2(before - m)
            total = stat[h][:, HD // 2 : HD // 2 + 1] * keep + jnp.sum(w, axis=-1, keepdims=True)
            mixed = acc[h] * keep + jnp.dot(
                w.astype(jnp.bfloat16), values, preferred_element_type=jnp.float32
            )
            done.append((mixed / total).reshape(width, GRP, HD))
        ox[:, p * 2 * GRP : (p + 1) * 2 * GRP, :] = jnp.concatenate(done, axis=1).astype(
            jnp.bfloat16
        )

    def r_copy(p, i, b, at):
        cut = pl.ds(p * 2 * GRP, 2 * GRP)
        return pltpu.make_async_remote_copy(
            src_ref=ox.at[pl.ds(b * cap, cap), cut], dst_ref=orx.at[pl.ds(at * cap, cap), cut],
            send_sem=rsend.at[p, i], recv_sem=rrecv.at[p, i],
            device_id={"branch": b}, device_id_type=MESH,
        )

    def give_back(p):
        def one(i, c):
            r_copy(p, i, lax.rem(me + i, n), me).start()
            return c

        lax.fori_loop(1, n, one, 0)

    for p in range(pairs):
        tail_pair(p)
        if p:
            give_back(p - 1)
    give_back(pairs - 1)
    own_r = pltpu.make_async_copy(part(ox, me), part(orx, me), lsem.at[2])
    own_r.start()

    def sent(i, c):
        b = lax.rem(me + i, n)
        x_copy(i, b, me).wait_send()
        m_copy(i, b, me).wait_send()
        return c

    lax.fori_loop(1, n, sent, 0)
    for e in range(res):
        spread(z, e, True, finish)

    def relayed(t, c):
        on_line(t, finish, False)
        off_line(t - 1, finish, False)
        return c

    lax.fori_loop(1, line, relayed, 0)
    off_line(line - 1, finish, False)

    def returned(i, c):
        for p in range(pairs):
            r_copy(p, i, lax.rem(me + n - i, n), lax.rem(me + n - i, n)).wait_recv()
        return c

    lax.fori_loop(1, n, returned, 0)
    own_r.wait()

    for r in range(0, count, some):
        for i in range(some):
            flat[i * heads : (i + 1) * heads] = orx[slot_of[r + i]].astype(jnp.float32)
        for h in range(heads):
            out_ref[r : r + some, h * HD : (h + 1) * HD] = flat[
                pl.ds(h, some, stride=heads), :
            ].astype(jnp.bfloat16)

    def gone(i, c):
        for p in range(pairs):
            r_copy(p, i, lax.rem(me + i, n), me).wait_send()
        return c

    lax.fori_loop(1, n, gone, 0)


def body(
    across, prompt_k, prompt_v, prompt_mask, shared_kv, shared_len, send_pick,
    unique_q, unique_kv, unique_owner,
):
    n = lax.axis_size("branch")
    rows = unique_q.shape[0]
    cap = 2 * rows // n
    width = n * cap
    res, rlen = shared_kv.shape[:2]
    heads = unique_q.shape[1] // HD
    kvh = unique_kv.shape[1] // (2 * HD)
    plen = prompt_k.shape[1]
    tail_n = -(-(n * rlen + width) // 128) * 128
    qrows = width * GRP
    vmem = pl.BlockSpec(memory_space=pltpu.VMEM)
    smem = pl.BlockSpec(memory_space=pltpu.SMEM)
    anyp = pl.BlockSpec(memory_space=pl.ANY)
    bf, f32 = jnp.bfloat16, jnp.float32
    dma = pltpu.SemaphoreType.DMA
    out = pl.pallas_call(
        functools.partial(kernel, n, across, cap, rlen, res, heads),
        out_shape=jax.ShapeDtypeStruct((rows, heads * HD), bf),
        in_specs=[smem, smem, smem, smem, vmem, vmem, vmem, anyp, anyp],
        out_specs=vmem,
        scratch_shapes=[
            pltpu.VMEM(prompt_k.shape[1:], bf),
            pltpu.VMEM(prompt_v.shape[1:], bf),
            pltpu.VMEM((max(min(rows, 16) * (heads + 2 * kvh), width * 2 * kvh), HD), f32),
            pltpu.VMEM((rows, heads + 2 * kvh, HD), bf),
            pltpu.SMEM((rows,), jnp.int32),
            pltpu.VMEM((1, plen), f32),
            pltpu.VMEM((n, 2 + cap, HD), jnp.int32),
            pltpu.VMEM((width, heads + 2 * kvh, HD), bf),
            pltpu.VMEM((width, heads + 2 * kvh, HD), bf),
            pltpu.VMEM((n, 2 + cap, HD), jnp.int32),
            pltpu.VMEM((n,) + shared_kv.shape, bf),
            pltpu.VMEM((tail_n, 2 * kvh * HD), bf),
            pltpu.VMEM((1, tail_n), jnp.int32),
            pltpu.VMEM((kvh, qrows, HD), f32),
            pltpu.VMEM((kvh, qrows, HD), f32),
            pltpu.VMEM((width, heads, HD), bf),
            pltpu.VMEM((width, heads, HD), bf),
            dma((2,)),
            dma((3,)),
            dma((n,)),
            dma((n,)),
            dma((n,)),
            dma((n,)),
            dma((2 + across, n * res)),
            dma((n * res,)),
            dma((kvh // 2, n)),
            dma((kvh // 2, n)),
        ],
        compiler_params=pltpu.CompilerParams(
            collective_id=0, has_side_effects=True, vmem_limit_bytes=67043328
        ),
    )(
        unique_owner.reshape(rows), send_pick, shared_len, prompt_mask,
        unique_q, unique_kv, shared_kv, prompt_k, prompt_v,
    )
    return out


def chips_across(mesh):
    devices = mesh.devices.reshape(-1, mesh.shape["branch"])[0]
    try:
        places = [tuple(d.coords) for d in devices[::2]]
    except (AttributeError, TypeError):
        return 1
    return sum(1 for p in places if p[2] == places[0][2])


def solution(mesh):
    spec1, spec2, spec3 = (P(("groups", "branch"), *(None,) * k) for k in range(3))
    in_specs = (spec3, spec3, spec2, spec3, spec1, spec2, spec2, spec2, spec2)
    return jax.shard_map(
        functools.partial(body, chips_across(mesh)),
        mesh=mesh, in_specs=in_specs, out_specs=spec2, check_vma=False,
    )
```

profile of v0, /device:TPU:0, one launch (start us, length us, event | category | flops | bytes accessed | tf_op | source)
XLA Modules:
  0.0 63.7 jit_solution(15987543220062219334)
XLA Ops:
  0.0 62.0 %shard_map.91 = bf16[16,8192]{1,0:T(8,128)(2,1)} custom-call(s32[16]{0:T(128)} %bitcast.1, s32[1,16]{1,0:T(1,128)} %pick_ref.1, s32[2]{0:T(128)} %len_ref.1, s32[1,8]{1,0:T(1,128)} %mask_ref.1, bf16[16,8192]{1,0:T(8,128)(2,1)} %q_ref.1, bf16[16,2048]{1,0:T(8,128)(2,1)} %kv_ref.1, bf16[2,24,2048]{2,1,0:T(8,128)(2,1)} %shared_ref.1, ...), custom_call_target="tpu_custom_call" | custom-call | tf_op jit(solution)/shard_map/pallas_call | solution.py:408
  62.1 1.7 %copy.11 = bf16[16,8192]{1,0:T(8,128)(2,1)} copy(bf16[16,8192]{1,0:T(8,128)(2,1)} %shard_map.91) | data formatting | bytes 524288
where the time goes:
time: 63.9 us; the launch traced here: 63.7 us
  Pallas kernels  62 us (97%)
  local copies, waits for them, and re-layouts  1.67 us (3%)
    pallas_call x1, Pallas kernels, body(): pl.pallas_call(functools.partial(kernel, n, across, cap, rlen, res, heads...  62 us
    unnamed x1, local copies, waits for them, and re-layouts  1.67 us

commit v1 on v0

v1 whole, which is shorter than its diff:
```python
import functools
import math

import jax
import jax.numpy as jnp
from jax import lax
from jax.experimental import pallas as pl
from jax.experimental.pallas import tpu as pltpu
from jax.sharding import PartitionSpec as P

HD = 128
GRP = 8
NEG = -1e30
MESH = pl.DeviceIdType.MESH


def kernel(
    n, across, cap, rlen, res, heads,
    owner_ref, pick_ref, len_ref, mask_ref, q_hbm, kv_hbm, shared_hbm, pk_hbm, pv_hbm,
    out_hbm,
    q_ref, kv_ref, pk, pv, flat, by_row, slot_of, pbias, meta_ref, xs, xr, mr, gath, tail, kslot,
    acc, stat, ox, out_ref,
    lsem, osem, xsend, xrecv, msend, mrecv, gsend, grecv, srecv, rsend, rrecv, *orx,
):
    me = lax.axis_index("branch")
    kvh = heads // GRP
    pairs = kvh // 2
    width = n * cap
    rows = width * GRP
    kvw = kvh * HD
    line = n // (2 * across)
    core = lax.rem(me, 2)
    chip = me // 2
    y = lax.rem(chip, across)
    z = chip // across
    sibling = me + 1 - 2 * core
    tail_n = tail.shape[0]
    scale = math.log2(math.e) / math.sqrt(HD)
    two = 2 * GRP
    barrier = pltpu.get_barrier_semaphore()

    def greet(i, c):
        pl.semaphore_signal(
            barrier, inc=1, device_id={"branch": lax.rem(me + i, n)}, device_id_type=MESH
        )
        return c

    lax.fori_loop(1, n, greet, 0)

    copy_s = pltpu.make_async_copy(shared_hbm, gath.at[me], lsem.at[0])
    copy_q = pltpu.make_async_copy(q_hbm, q_ref, lsem.at[1])
    copy_u = pltpu.make_async_copy(kv_hbm, kv_ref, lsem.at[2])
    copy_k = pltpu.make_async_copy(pk_hbm.at[0], pk, lsem.at[3])
    copy_v = pltpu.make_async_copy(pv_hbm.at[0], pv, lsem.at[4])
    copy_s.start()
    copy_q.start()
    copy_u.start()
    copy_k.start()
    copy_v.start()

    def ship(source, e, target, recv):
        return pltpu.make_async_remote_copy(
            src_ref=gath.at[source, e], dst_ref=gath.at[source, e],
            send_sem=gsend.at[0], recv_sem=recv,
            device_id={"branch": target}, device_id_type=MESH,
        )

    def slot(source, e):
        return grecv.at[(source // 2) * res + e]

    def member(zz, yy, cc):
        return (zz * across + yy) * 2 + cc

    def spread(zs, e, act):
        source = member(zs, y, core)
        recv = slot(source, e)

        @pl.when(jnp.logical_and(zs <= z, z + 1 < line))
        def _():
            act(ship(source, e, member(lax.rem(z + 1, line), y, core), recv))

        @pl.when(jnp.logical_and(zs >= z, z >= 1))
        def _():
            act(ship(source, e, member(lax.rem(z + line - 1, line), y, core), recv))

        for d in range(1, across):
            act(ship(source, e, member(z, lax.rem(y + d, across), core), recv))
        act(ship(source, e, sibling, srecv.at[0]))

    def arrived(source, e):
        ship(source, e, sibling, slot(source, e)).wait_recv()

    begin = lambda copy: copy.start()
    finish = lambda copy: copy.wait_send()

    def on_line(t, act, waits):
        for e in range(res):
            for up in (0, 1):
                zs = z - t if up == 0 else z + t
                ok = zs >= 0 if up == 0 else zs < line

                @pl.when(ok)
                def _():
                    zc = lax.rem(zs + line, line)
                    if waits:
                        arrived(member(zc, y, core), e)
                    spread(zc, e, act)

    def cross(zs, act, waits):
        for d in range(1, across):
            source = member(zs, lax.rem(y + d, across), core)
            for e in range(res):
                if waits:
                    arrived(source, e)
                act(ship(source, e, sibling, srecv.at[0]))

    def off_line(t, act, waits):
        @pl.when(z - t >= 0)
        def _():
            cross(lax.rem(z - t + line, line), act, waits)

        @pl.when(jnp.logical_and(z + t < line, t > 0))
        def _():
            cross(lax.rem(z + t, line), act, waits)

    cuts = [1 + (line - 1) * j // 3 for j in range(4)]

    def on_lines(j):
        def one(t, c):
            on_line(t, begin, True)
            return c

        lax.fori_loop(cuts[j], cuts[j + 1], one, 0)

    def off_lines(j):
        def one(t, c):
            off_line(t, begin, True)
            return c

        if across > 1:
            lax.fori_loop(cuts[j] if j >= 0 else 0, cuts[j + 1], one, 0)

    def group(g):
        lo = 0 if g == 0 else g * two + 2 * kvh
        return slice(lo, (g + 1) * two + 2 * kvh)

    def x_copy(g, b, at):
        return pltpu.make_async_remote_copy(
            src_ref=xs.at[pl.ds(b * cap, cap), group(g)],
            dst_ref=xr.at[pl.ds(at * cap, cap), group(g)],
            send_sem=xsend.at[0], recv_sem=xrecv.at[g],
            device_id={"branch": b}, device_id_type=MESH,
        )

    def m_copy(b, at):
        return pltpu.make_async_remote_copy(
            src_ref=meta_ref.at[b], dst_ref=mr.at[at],
            send_sem=msend.at[0], recv_sem=mrecv.at[0],
            device_id={"branch": b}, device_id_type=MESH,
        )

    def send_x(g):
        def one(i, c):
            b = lax.rem(me + i, n)
            x_copy(g, b, me).start()
            if g == 0:
                m_copy(b, me).start()
            return c

        lax.fori_loop(1, n, one, 0)

    others = pl.ds(0, (n - 1) * cap)

    def x_all(g):
        return pltpu.make_async_remote_copy(
            src_ref=xs.at[others, group(g)], dst_ref=xr.at[others, group(g)],
            send_sem=xsend.at[0], recv_sem=xrecv.at[g],
            device_id={"branch": sibling}, device_id_type=MESH,
        )

    def m_all():
        return pltpu.make_async_remote_copy(
            src_ref=meta_ref.at[pl.ds(0, n - 1)], dst_ref=mr.at[pl.ds(0, n - 1)],
            send_sem=msend.at[0], recv_sem=mrecv.at[0],
            device_id={"branch": sibling}, device_id_type=MESH,
        )

    def sib_all():
        half = gath.at[pl.ds(0, n // 2)]
        return pltpu.make_async_remote_copy(
            src_ref=half, dst_ref=half, send_sem=gsend.at[0], recv_sem=srecv.at[0],
            device_id={"branch": sibling}, device_id_type=MESH,
        )

    copy_s.wait()
    pl.semaphore_wait(barrier, n - 1)
    for e in range(res):
        spread(z, e, begin)

    count = q_ref.shape[0]
    per = heads + 2 * kvh
    some = min(count, 16)

    def number(j, c):
        mine = owner_ref[j]
        rank = lax.fori_loop(
            0, j, lambda i, r: r + jnp.where(owner_ref[i] == mine, 1, 0), jnp.int32(0)
        )
        slot_of[j] = mine * cap + rank
        return c

    lax.fori_loop(0, count, number, 0)
    copy_q.wait()
    copy_u.wait()

    for r in range(0, count, some):
        for h in range(per):
            ref, g = (q_ref, h) if h < heads else (kv_ref, h - heads)
            at = h if h < two else h + 2 * kvh if h < heads else two + g
            flat[pl.ds(at, some, stride=per), :] = ref[
                r : r + some, g * HD : (g + 1) * HD
            ].astype(jnp.float32)
        for i in range(some):
            by_row[r + i] = flat[i * per : (i + 1) * per].astype(jnp.bfloat16)

    lane = lax.broadcasted_iota(jnp.int32, (1, HD), 1)

    def place(b, c):
        def scan(r, found):
            for u in range(some):
                i = r * some + u
                hit = owner_ref[i] == b
                rows_at, seen = found[:cap], found[cap]
                rows_at = [
                    jnp.where(jnp.logical_and(hit, seen == k), i, at)
                    for k, at in enumerate(rows_at)
                ]
                found = (*rows_at, seen + jnp.where(hit, 1, 0))
            return found

        found = lax.fori_loop(0, count // some, scan, (jnp.int32(0),) * (cap + 1))
        pick = pick_ref[0, b]
        length = jnp.int32(0)
        for e in range(res):
            length = jnp.where(pick == e, len_ref[e], length)
        meta_ref[b] = jnp.where(
            lane == 0, pick, jnp.where(lane == 1, length, jnp.where(found[cap] > lane - 2, 1, 0))
        )
        for k in range(cap):
            xs[b * cap + k] = by_row[found[k]]
        return c

    lax.fori_loop(0, n, place, 0)
    blocks = mask_ref.shape[1]
    block = pk.shape[0] // blocks
    for g in range(blocks):
        pbias[:, g * block : (g + 1) * block] = jnp.full(
            (1, block), jnp.where(mask_ref[0, g] > 0, 0.0, NEG), jnp.float32
        )

    def part(ref, b):
        return ref.at[pl.ds(b * cap, cap)]

    own_x = pltpu.make_async_copy(part(xs, me), part(xr, me), lsem.at[5])
    own_m = pltpu.make_async_copy(meta_ref.at[me], mr.at[me], lsem.at[6])

    def queries(p):
        lo = 0 if p == 0 else p * two + 2 * kvh
        both = xr[:, lo : lo + two, :].astype(jnp.float32)
        return [
            both[:, k * GRP : (k + 1) * GRP].reshape(rows, HD).astype(jnp.bfloat16)
            for k in range(2)
        ]

    def scores(q, k):
        return lax.dot_general(q, k, (((1,), (1,)), ((), ())), preferred_element_type=jnp.float32)

    half = lax.broadcasted_iota(jnp.int32, (rows, HD), 1) < HD // 2

    def prompt_pair(p):
        for k, q in enumerate(queries(p)):
            h = 2 * p + k
            cols = slice(h * HD, (h + 1) * HD)
            s = scores(q, pk[:, cols]) * scale + pbias[...]
            m = jnp.max(s, axis=-1, keepdims=True)
            w = jnp.exp2(s - m)
            stat[h] = jnp.where(half, m, jnp.sum(w, axis=-1, keepdims=True))
            acc[h] = jnp.dot(
                w.astype(jnp.bfloat16), pv[:, cols], preferred_element_type=jnp.float32
            )

    def tail_keys():
        kv_at = slice(two, two + 2 * kvh)
        flat[: width * 2 * kvh] = (
            xr[:, kv_at, :].astype(jnp.float32).reshape(width * 2 * kvh, HD)
        )
        for j in range(2 * kvh):
            tail[n * rlen : n * rlen + width, j * HD : (j + 1) * HD] = flat[
                pl.ds(j, width, stride=2 * kvh), :
            ].astype(jnp.bfloat16)
        col = lax.broadcasted_iota(jnp.int32, (1, tail_n), 1)

        def limits(s, carry):
            length, live = carry
            meta = mr[s]
            length = jnp.where(col // rlen == s, meta[:, 1:2], length)
            for k in range(cap):
                live = jnp.where(col == n * rlen + s * cap + k, meta[:, 2 + k : 3 + k], live)
            return length, live

        zero = jnp.zeros((1, tail_n), jnp.int32)
        length, live = lax.fori_loop(0, n, limits, (zero, zero))
        shared_ok = jnp.logical_and(col < n * rlen, lax.rem(col, rlen) < length)
        kslot[...] = jnp.where(shared_ok, -1, jnp.where(live > 0, col - n * rlen, width))

    row_slot = lax.broadcasted_iota(jnp.int32, (rows, 1), 0) // GRP

    def choose(t, c):
        two_of = []
        for s in (2 * t, 2 * t + 1):
            pick = mr[s][:, 0:1]
            chosen = gath[s, 0].astype(jnp.float32)
            for e in range(1, res):
                chosen = jnp.where(pick == e, gath[s, e].astype(jnp.float32), chosen)
            two_of.append(chosen)
        tail[pl.ds(pl.multiple_of(t * 2 * rlen, 16), 2 * rlen), :] = jnp.concatenate(
            two_of, axis=0
        ).astype(jnp.bfloat16)
        return c

    def tail_pair(p):
        done = []
        for k, q in enumerate(queries(p)):
            h = 2 * p + k
            keys = tail[:, h * HD : (h + 1) * HD]
            values = tail[:, kvw + h * HD : kvw + (h + 1) * HD]
            s = jnp.where(kslot[...] <= row_slot, scores(q, keys) * scale, NEG)
            before = stat[h][:, :1]
            m = jnp.maximum(before, jnp.max(s, axis=-1, keepdims=True))
            w = jnp.exp2(s - m)
            keep = jnp.exp2(before - m)
            total = stat[h][:, HD // 2 : HD // 2 + 1] * keep + jnp.sum(w, axis=-1, keepdims=True)
            mixed = acc[h] * keep + jnp.dot(
                w.astype(jnp.bfloat16), values, preferred_element_type=jnp.float32
            )
            done.append((mixed / total).reshape(width, GRP, HD))
        ox[:, p * two : (p + 1) * two, :] = jnp.concatenate(done, axis=1).astype(jnp.bfloat16)

    def r_copy(p, b, at):
        cut = slice(p * two, (p + 1) * two)
        return pltpu.make_async_remote_copy(
            src_ref=ox.at[pl.ds(b * cap, cap), cut], dst_ref=orx[p].at[pl.ds(at * cap, cap)],
            send_sem=rsend.at[0], recv_sem=rrecv.at[p],
            device_id={"branch": b}, device_id_type=MESH,
        )

    def r_all(p):
        cut = slice(p * two, (p + 1) * two)
        return pltpu.make_async_remote_copy(
            src_ref=ox.at[others, cut], dst_ref=orx[p].at[others],
            send_sem=rsend.at[0], recv_sem=rrecv.at[p],
            device_id={"branch": sibling}, device_id_type=MESH,
        )

    def own_r(p):
        cut = slice(p * two, (p + 1) * two)
        return pltpu.make_async_copy(
            ox.at[pl.ds(me * cap, cap), cut], orx[p].at[pl.ds(me * cap, cap)], osem.at[p]
        )

    def give_back(p):
        def one(i, c):
            r_copy(p, lax.rem(me + i, n), me).start()
            return c

        lax.fori_loop(1, n, one, 0)
        own_r(p).start()

    def prompt(p):
        x_all(p).wait_recv()
        if p == 0:
            m_all().wait_recv()
            own_x.wait()
            own_m.wait()
            copy_k.wait()
            copy_v.wait()
        prompt_pair(p)

    def put(p):
        cols = slice(p * two * HD, (p + 1) * two * HD)
        return pltpu.make_async_copy(
            out_ref.at[:, cols], out_hbm.at[:, cols], osem.at[pairs + p]
        )

    own_x.start()
    own_m.start()
    on_lines(0)
    send_x(0)
    tail[...] = jnp.zeros_like(tail)
    off_lines(-1)
    on_lines(1)
    send_x(1)
    for g in range(2, pairs - 1):
        send_x(g)
    off_lines(0)
    on_lines(2)
    send_x(pairs - 1)
    prompt(0)
    tail_keys()
    off_lines(1)
    for p in range(1, pairs - 1):
        prompt(p)
    off_lines(2)
    sib_all().wait_recv()
    lax.fori_loop(0, n // 2, choose, 0)
    for p in range(pairs):
        if p == pairs - 1:
            prompt(p)
        tail_pair(p)
        give_back(p)

    for g in range(pairs):
        x_all(g).wait_send()
    m_all().wait_send()
    for e in range(res):
        spread(z, e, finish)

    def relayed(t, c):
        on_line(t, finish, False)
        return c

    lax.fori_loop(1, line, relayed, 0)

    def crossed(t, c):
        off_line(t, finish, False)
        return c

    if across > 1:
        lax.fori_loop(0, line, crossed, 0)

    for p in range(pairs):
        r_all(p).wait_recv()
        own_r(p).wait()
        for r in range(0, count, some):
            for i in range(some):
                flat[i * two : (i + 1) * two] = orx[p][slot_of[r + i]].astype(jnp.float32)
            for h in range(two):
                at = (p * two + h) * HD
                out_ref[r : r + some, at : at + HD] = flat[
                    pl.ds(h, some, stride=two), :
                ].astype(jnp.bfloat16)
        put(p).start()
    for p in range(pairs):
        r_all(p).wait_send()
    for p in range(pairs):
        put(p).wait()


def body(
    across, prompt_k, prompt_v, prompt_mask, shared_kv, shared_len, send_pick,
    unique_q, unique_kv, unique_owner,
):
    n = lax.axis_size("branch")
    rows = unique_q.shape[0]
    cap = 2 * rows // n
    width = n * cap
    res, rlen = shared_kv.shape[:2]
    heads = unique_q.shape[1] // HD
    kvh = unique_kv.shape[1] // (2 * HD)
    pairs = kvh // 2
    plen = prompt_k.shape[1]
    tail_n = -(-(n * rlen + width) // 128) * 128
    qrows = width * GRP
    smem = pl.BlockSpec(memory_space=pltpu.SMEM)
    anyp = pl.BlockSpec(memory_space=pl.ANY)
    bf, f32 = jnp.bfloat16, jnp.float32
    dma = pltpu.SemaphoreType.DMA
    out = pl.pallas_call(
        functools.partial(kernel, n, across, cap, rlen, res, heads),
        out_shape=jax.ShapeDtypeStruct((rows, heads * HD), bf),
        in_specs=[smem, smem, smem, smem, anyp, anyp, anyp, anyp, anyp],
        out_specs=anyp,
        scratch_shapes=[
            pltpu.VMEM(unique_q.shape, bf),
            pltpu.VMEM(unique_kv.shape, bf),
            pltpu.VMEM(prompt_k.shape[1:], bf),
            pltpu.VMEM(prompt_v.shape[1:], bf),
            pltpu.VMEM((max(min(rows, 16) * (heads + 2 * kvh), width * 2 * kvh), HD), f32),
            pltpu.VMEM((rows, heads + 2 * kvh, HD), bf),
            pltpu.SMEM((rows,), jnp.int32),
            pltpu.VMEM((1, plen), f32),
            pltpu.VMEM((n, 1, HD), jnp.int32),
            pltpu.VMEM((width, heads + 2 * kvh, HD), bf),
            pltpu.VMEM((width, heads + 2 * kvh, HD), bf),
            pltpu.VMEM((n, 1, HD), jnp.int32),
            pltpu.VMEM((n,) + shared_kv.shape, bf),
            pltpu.VMEM((tail_n, 2 * kvh * HD), bf),
            pltpu.VMEM((1, tail_n), jnp.int32),
            pltpu.VMEM((kvh, qrows, HD), f32),
            pltpu.VMEM((kvh, qrows, HD), f32),
            pltpu.VMEM((width, heads, HD), bf),
            pltpu.VMEM((rows, heads * HD), bf),
            dma((7,)),
            dma((2 * pairs,)),
            dma((1,)),
            dma((pairs,)),
            dma((1,)),
            dma((1,)),
            dma((1,)),
            dma((n // 2 * res,)),
            dma((1,)),
            dma((1,)),
            dma((pairs,)),
            *[pltpu.VMEM((width, 2 * GRP, HD), bf)] * pairs,
        ],
        compiler_params=pltpu.CompilerParams(
            collective_id=0, has_side_effects=True, vmem_limit_bytes=67043328
        ),
    )(
        unique_owner.reshape(rows), send_pick, shared_len, prompt_mask,
        unique_q, unique_kv, shared_kv, prompt_k, prompt_v,
    )
    return out


def chips_across(mesh):
    devices = mesh.devices.reshape(-1, mesh.shape["branch"])[0]
    try:
        places = [tuple(d.coords) for d in devices[::2]]
    except (AttributeError, TypeError):
        return 1
    return sum(1 for p in places if p[2] == places[0][2])


def solution(mesh):
    spec1, spec2, spec3 = (P(("groups", "branch"), *(None,) * k) for k in range(3))
    in_specs = (spec3, spec3, spec2, spec3, spec1, spec2, spec2, spec2, spec2)
    return jax.shard_map(
        functools.partial(body, chips_across(mesh)),
        mesh=mesh, in_specs=in_specs, out_specs=spec2, check_vma=False,
    )
```

time: 63.9 us -> 51.8 us (0.81)
  Pallas kernels: 62 us -> 49.9 us
    pallas_call x1, Pallas kernels: 62 us -> 49.9 us  [body(): pl.pallas_call(functools.partial(kernel, n, across, cap, rlen, res, heads...]
where the time goes in v1:
time: 51.8 us; the launch traced here: 51.6 us
  Pallas kernels  49.9 us (96%)
  local copies, waits for them, and re-layouts  1.67 us (3%)
    pallas_call x1, Pallas kernels, body(): pl.pallas_call(functools.partial(kernel, n, across, cap, rlen, res, heads...  49.9 us
    unnamed x1, local copies, waits for them, and re-layouts  1.67 us

profile of v1, /device:TPU:0, one launch (start us, length us, event | category | flops | bytes accessed | tf_op | source)
XLA Modules:
  0.0 51.6 jit_solution(11720054460199793722)
XLA Ops:
  0.0 49.9 %shard_map.91 = bf16[16,8192]{1,0:T(8,128)(2,1)} custom-call(s32[16]{0:T(128)} %bitcast.1, s32[1,16]{1,0:T(1,128)} %pick_ref.1, s32[2]{0:T(128)} %len_ref.1, s32[1,8]{1,0:T(1,128)} %mask_ref.1, bf16[16,8192]{1,0:T(8,128)(2,1)} %q_hbm.1, bf16[16,2048]{1,0:T(8,128)(2,1)} %kv_hbm.1, bf16[2,24,2048]{2,1,0:T(8,128)(2,1)} %shared_hbm.1, ...), custom_call_target="tpu_custom_call" | custom-call | tf_op jit(solution)/shard_map/pallas_call | solution.py:478
  49.9 1.7 %copy.11 = bf16[16,8192]{1,0:T(8,128)(2,1)} copy(bf16[16,8192]{1,0:T(8,128)(2,1)} %shard_map.91) | data formatting | bytes 524288

commit v2 on v1

v2 whole, which is shorter than its diff:
```python
import functools
import math

import jax
import jax.numpy as jnp
from jax import lax
from jax.experimental import pallas as pl
from jax.experimental.pallas import tpu as pltpu
from jax.sharding import PartitionSpec as P

HD = 128
GRP = 8
NEG = -1e30
MESH = pl.DeviceIdType.MESH


def kernel(
    n, across, cap, rlen, res, heads,
    owner_hbm, pick_hbm, len_hbm, mask_hbm, q_hbm, kv_hbm, shared_hbm, pk_hbm, pv_hbm,
    out_ref,
    owner_ref, pick_ref, len_ref, mask_ref, meta_in,
    q_ref, kv_ref, pk, pv, flat, by_row, slot_of, pbias, tbias, meta_ref, xs, xr, mr, tail, kslot,
    ox, lsem, osem, xsend, xrecv, msend, mrecv, gsend, grecv, srecv, rsend, rrecv, *by_group,
):
    me = lax.axis_index("branch")
    kvh = heads // GRP
    pairs = kvh // 2
    orx, gath = by_group[:pairs], by_group[pairs:]
    width = n * cap
    rows = width * GRP
    kvw = kvh * HD
    line = n // (2 * across)
    core = lax.rem(me, 2)
    chip = me // 2
    y = lax.rem(chip, across)
    z = chip // across
    sibling = me + 1 - 2 * core
    tail_n = tail.shape[1]
    scale = math.log2(math.e) / math.sqrt(HD)
    two = 2 * GRP
    barrier = pltpu.get_barrier_semaphore()

    def greet(i, c):
        pl.semaphore_signal(
            barrier, inc=1, device_id={"branch": lax.rem(me + i, n)}, device_id_type=MESH
        )
        return c

    lax.fori_loop(1, n, greet, 0)

    gw = 2 * HD

    def load_shared(g, part):
        return pltpu.make_async_copy(
            shared_hbm.at[:, :, pl.ds(part * kvw + g * gw, gw)],
            gath[g].at[me, :, :, pl.ds(part * gw, gw)],
            lsem.at[9 + g],
        )

    copy_q = pltpu.make_async_copy(q_hbm, q_ref, lsem.at[4])
    copy_u = pltpu.make_async_copy(kv_hbm, kv_ref, lsem.at[5])
    copy_k = pltpu.make_async_copy(pk_hbm.at[0], pk, lsem.at[6])
    copy_v = pltpu.make_async_copy(pv_hbm.at[0], pv, lsem.at[7])
    for g in range(pairs):
        for part in range(2):
            load_shared(g, part).start()
    small = [
        pltpu.make_async_copy(src, dst, lsem.at[i])
        for i, (src, dst) in enumerate(
            [(owner_hbm, owner_ref), (pick_hbm, pick_ref), (len_hbm, len_ref), (mask_hbm, mask_ref)]
        )
    ]
    for copy in small:
        copy.start()
    copy_q.start()
    copy_u.start()
    copy_k.start()
    copy_v.start()

    def ship(source, g, target, recv):
        return pltpu.make_async_remote_copy(
            src_ref=gath[g].at[source], dst_ref=gath[g].at[source],
            send_sem=gsend.at[0], recv_sem=recv,
            device_id={"branch": target}, device_id_type=MESH,
        )

    def slot(source, g):
        return grecv.at[(source // 2) * pairs + g]

    def member(zz, yy, cc):
        return (zz * across + yy) * 2 + cc

    def spread(zs, g, act):
        source = member(zs, y, core)
        recv = slot(source, g)

        @pl.when(jnp.logical_and(zs <= z, z + 1 < line))
        def _():
            act(ship(source, g, member(lax.rem(z + 1, line), y, core), recv))

        @pl.when(jnp.logical_and(zs >= z, z >= 1))
        def _():
            act(ship(source, g, member(lax.rem(z + line - 1, line), y, core), recv))

        for d in range(1, across):
            act(ship(source, g, member(z, lax.rem(y + d, across), core), recv))
        act(ship(source, g, sibling, srecv.at[g]))

    def arrived(source, g):
        ship(source, g, sibling, slot(source, g)).wait_recv()

    begin = lambda copy: copy.start()
    finish = lambda copy: copy.wait_send()

    def on_line(t, g, act, waits):
        for up in (0, 1):
            zs = z - t if up == 0 else z + t
            ok = zs >= 0 if up == 0 else zs < line

            @pl.when(ok)
            def _():
                zc = lax.rem(zs + line, line)
                if waits:
                    arrived(member(zc, y, core), g)
                spread(zc, g, act)

    def cross(zs, g, act, waits):
        for d in range(1, across):
            source = member(zs, lax.rem(y + d, across), core)
            if waits:
                arrived(source, g)
            act(ship(source, g, sibling, srecv.at[g]))

    def off_line(t, g, act, waits):
        @pl.when(z - t >= 0)
        def _():
            cross(lax.rem(z - t + line, line), g, act, waits)

        @pl.when(jnp.logical_and(z + t < line, t > 0))
        def _():
            cross(lax.rem(z + t, line), g, act, waits)

    cuts = [0] + [1 + (line - 1) * j // 3 for j in range(4)]

    def own(g):
        spread(z, g, begin)

    def on_lines(g, j):
        def one(t, c):
            on_line(t, g, begin, True)
            return c

        lax.fori_loop(cuts[j], cuts[j + 1], one, 0)

    def off_lines(g, j):
        def one(t, c):
            off_line(t, g, begin, True)
            return c

        if across > 1:
            lax.fori_loop(cuts[j], cuts[j + 1], one, 0)

    def group(g):
        lo = 0 if g == 0 else g * two + 2 * kvh
        return slice(lo, (g + 1) * two + 2 * kvh)

    def x_copy(g, b, at):
        return pltpu.make_async_remote_copy(
            src_ref=xs.at[pl.ds(b * cap, cap), group(g)],
            dst_ref=xr.at[pl.ds(at * cap, cap), group(g)],
            send_sem=xsend.at[0], recv_sem=xrecv.at[g],
            device_id={"branch": b}, device_id_type=MESH,
        )

    def m_copy(b, at):
        return pltpu.make_async_remote_copy(
            src_ref=meta_ref.at[b], dst_ref=mr.at[at],
            send_sem=msend.at[0], recv_sem=mrecv.at[0],
            device_id={"branch": b}, device_id_type=MESH,
        )

    def send_to(g, b):
        x_copy(g, b, me).start()
        if g == 0:
            m_copy(b, me).start()

    def send_x(g, d):
        def one(i, c):
            at = lax.rem(2 * z + core + i, 2 * line)
            send_to(g, member(at // 2, lax.rem(y + d, across), lax.rem(at, 2)))
            return c

        lax.fori_loop(0 if d else 1, 2 * line, one, 0)

    def send_near(g):
        send_x(g, 0)

    def send_far(g):
        for d in range(1, across):
            send_x(g, d)

    others = pl.ds(0, (n - 1) * cap)

    def x_all(g):
        return pltpu.make_async_remote_copy(
            src_ref=xs.at[others, group(g)], dst_ref=xr.at[others, group(g)],
            send_sem=xsend.at[0], recv_sem=xrecv.at[g],
            device_id={"branch": sibling}, device_id_type=MESH,
        )

    def m_all():
        return pltpu.make_async_remote_copy(
            src_ref=meta_ref.at[pl.ds(0, n - 1)], dst_ref=mr.at[pl.ds(0, n - 1)],
            send_sem=msend.at[0], recv_sem=mrecv.at[0],
            device_id={"branch": sibling}, device_id_type=MESH,
        )

    def sib_all(g):
        half = gath[g].at[pl.ds(0, n // 2)]
        return pltpu.make_async_remote_copy(
            src_ref=half, dst_ref=half, send_sem=gsend.at[0], recv_sem=srecv.at[g],
            device_id={"branch": sibling}, device_id_type=MESH,
        )

    def loaded(g):
        mine = gath[g].at[me]
        pltpu.make_async_copy(mine, mine, lsem.at[9 + g]).wait()

    loaded(0)
    pl.semaphore_wait(barrier, n - 1)
    own(0)
    for g in range(1, pairs):
        loaded(g)
        own(g)
    for copy in small:
        copy.wait()
    count = q_ref.shape[0]
    per = heads + 2 * kvh
    some = min(count, 16)

    def number(j, c):
        mine = owner_ref[j]
        rank = lax.fori_loop(
            0, j, lambda i, r: r + jnp.where(owner_ref[i] == mine, 1, 0), jnp.int32(0)
        )
        slot_of[j] = mine * cap + rank
        return c

    lax.fori_loop(0, count, number, 0)
    copy_q.wait()
    copy_u.wait()

    for r in range(0, count, some):
        for h in range(per):
            ref, g = (q_ref, h) if h < heads else (kv_ref, h - heads)
            at = h if h < two else h + 2 * kvh if h < heads else two + g
            flat[pl.ds(at, some, stride=per), :] = ref[
                r : r + some, g * HD : (g + 1) * HD
            ].astype(jnp.float32)
        for i in range(some):
            by_row[r + i] = flat[i * per : (i + 1) * per].astype(jnp.bfloat16)

    lane = lax.broadcasted_iota(jnp.int32, (1, HD), 1)

    def place(b, c):
        def scan(r, found):
            for u in range(some):
                i = r * some + u
                hit = owner_ref[i] == b
                rows_at, seen = found[:cap], found[cap]
                rows_at = [
                    jnp.where(jnp.logical_and(hit, seen == k), i, at)
                    for k, at in enumerate(rows_at)
                ]
                found = (*rows_at, seen + jnp.where(hit, 1, 0))
            return found

        found = lax.fori_loop(0, count // some, scan, (jnp.int32(0),) * (cap + 1))
        pick = pick_ref[0, b]
        length = jnp.int32(0)
        for e in range(res):
            length = jnp.where(pick == e, len_ref[e], length)
        meta_ref[b] = jnp.where(
            lane == 0, pick, jnp.where(lane == 1, length, jnp.where(found[cap] > lane - 2, 1, 0))
        )
        for k in range(cap):
            xs[b * cap + k] = by_row[found[k]]
        return c

    lax.fori_loop(0, n, place, 0)
    blocks = mask_ref.shape[1]
    block = pk.shape[0] // blocks
    for g in range(blocks):
        pbias[:, g * block : (g + 1) * block] = jnp.full(
            (1, block), jnp.where(mask_ref[0, g] > 0, 0.0, NEG), jnp.float32
        )

    def part(ref, b):
        return ref.at[pl.ds(b * cap, cap)]

    own_x = pltpu.make_async_copy(part(xs, me), part(xr, me), osem.at[pairs])
    own_m = pltpu.make_async_copy(meta_ref.at[me], mr.at[me], osem.at[pairs + 1])

    def queries(p):
        lo = 0 if p == 0 else p * two + 2 * kvh
        both = xr[:, lo : lo + two, :].astype(jnp.float32)
        return [
            both[:, k * GRP : (k + 1) * GRP].reshape(rows, HD).astype(jnp.bfloat16)
            for k in range(2)
        ]

    def scores(q, k):
        return lax.dot_general(q, k, (((1,), (1,)), ((), ())), preferred_element_type=jnp.float32)

    copy_m = pltpu.make_async_copy(mr, meta_in, osem.at[pairs + 2])

    def metas():
        m_all().wait_recv()
        own_m.wait()
        copy_m.start()

    def tail_keys():
        copy_m.wait()
        col = lax.broadcasted_iota(jnp.int32, (1, tail_n), 1)
        owner, at_row = col // rlen, lax.rem(col, rlen)
        some_s = min(n, 16)

        def limits(i, carry):
            length, live = carry
            for u in range(some_s):
                s = i * some_s + u
                length = jnp.where(owner == s, meta_in[s, 0, 1], length)
                for k in range(cap):
                    live = jnp.where(
                        col == n * rlen + s * cap + k, meta_in[s, 0, 2 + k], live
                    )
            return length, live

        zero = jnp.zeros((1, tail_n), jnp.int32)
        length, live = lax.fori_loop(0, n // some_s, limits, (zero, zero))
        shared_ok = jnp.logical_and(col < n * rlen, at_row < length)
        tbias[...] = jnp.where(shared_ok, 0.0, NEG)
        kslot[...] = jnp.where(shared_ok, -1, jnp.where(live > 0, col - n * rlen, width))
        x_all(0).wait_recv()
        own_x.wait()
        kv_at = slice(two, two + 2 * kvh)
        flat[: width * 2 * kvh] = (
            xr[:, kv_at, :].astype(jnp.float32).reshape(width * 2 * kvh, HD)
        )
        for j in range(2 * kvh):
            at = j % 2 + 2 * (j // kvh)
            tail[j % kvh // 2, n * rlen : n * rlen + width, at * HD : (at + 1) * HD] = flat[
                pl.ds(j, width, stride=2 * kvh), :
            ].astype(jnp.bfloat16)

    row_slot = lax.broadcasted_iota(jnp.int32, (rows, 1), 0) // GRP
    fixed = n * rlen // HD * HD

    def choose(g):
        sib_all(g).wait_recv()
        block = min(n, 16)

        def one(i, c):
            for t in range(0, block, 2):
                two_of = [
                    gath[g][s, jnp.maximum(meta_in[s, 0, 0], 0)].astype(jnp.float32)
                    for s in (i * block + t, i * block + t + 1)
                ]
                at = pl.multiple_of(i * block * rlen + t * rlen, 16)
                tail[g, pl.ds(at, 2 * rlen), :] = jnp.concatenate(two_of, axis=0).astype(
                    jnp.bfloat16
                )
            return c

        lax.fori_loop(0, n // block, one, 0)

    def attend(p):
        if p == 0:
            copy_k.wait()
            copy_v.wait()
        else:
            x_all(p).wait_recv()
        done = []
        for k, q in enumerate(queries(p)):
            h = 2 * p + k
            cols = slice(h * HD, (h + 1) * HD)
            keys = tail[p, :, k * HD : (k + 1) * HD]
            values = tail[p, :, (2 + k) * HD : (3 + k) * HD]
            sp = scores(q, pk[:, cols]) * scale + pbias[...]
            st = scores(q, keys) * scale
            sf = st[:, :fixed] + tbias[:, :fixed]
            su = jnp.where(kslot[:, fixed:] <= row_slot, st[:, fixed:], NEG)
            m = jnp.maximum(
                jnp.max(sp, axis=-1, keepdims=True),
                jnp.maximum(
                    jnp.max(sf, axis=-1, keepdims=True), jnp.max(su, axis=-1, keepdims=True)
                ),
            )
            wp = jnp.exp2(sp - m)
            wt = jnp.exp2(jnp.concatenate([sf, su], axis=1) - m)
            total = jnp.sum(wp, axis=-1, keepdims=True) + jnp.sum(wt, axis=-1, keepdims=True)
            mixed = jnp.dot(
                wp.astype(jnp.bfloat16), pv[:, cols], preferred_element_type=jnp.float32
            ) + jnp.dot(wt.astype(jnp.bfloat16), values, preferred_element_type=jnp.float32)
            done.append((mixed / total).reshape(width, GRP, HD))
        ox[:, p * two : (p + 1) * two, :] = jnp.concatenate(done, axis=1).astype(jnp.bfloat16)

    def r_copy(p, b, at):
        cut = slice(p * two, (p + 1) * two)
        return pltpu.make_async_remote_copy(
            src_ref=ox.at[pl.ds(b * cap, cap), cut], dst_ref=orx[p].at[pl.ds(at * cap, cap)],
            send_sem=rsend.at[0], recv_sem=rrecv.at[p],
            device_id={"branch": b}, device_id_type=MESH,
        )

    def r_all(p):
        cut = slice(p * two, (p + 1) * two)
        return pltpu.make_async_remote_copy(
            src_ref=ox.at[others, cut], dst_ref=orx[p].at[others],
            send_sem=rsend.at[0], recv_sem=rrecv.at[p],
            device_id={"branch": sibling}, device_id_type=MESH,
        )

    def own_r(p):
        cut = slice(p * two, (p + 1) * two)
        return pltpu.make_async_copy(
            ox.at[pl.ds(me * cap, cap), cut], orx[p].at[pl.ds(me * cap, cap)], osem.at[p]
        )

    def give_back(p):
        def one(i, c):
            r_copy(p, lax.rem(me + i, n), me).start()
            return c

        lax.fori_loop(1, n, one, 0)
        own_r(p).start()

    own_x.start()
    own_m.start()
    on_lines(0, 1)
    on_lines(1, 1)
    on_lines(2, 1)
    on_lines(3, 1)
    used = n * rlen + width
    if used < tail_n:
        tail[:, used:, :] = jnp.zeros((pairs, tail_n - used, 4 * HD), jnp.bfloat16)
    send_near(0)
    send_far(0)
    on_lines(0, 2)
    on_lines(1, 2)
    on_lines(2, 2)
    on_lines(3, 2)
    send_near(1)
    send_far(1)
    send_near(2)
    send_far(2)
    for j in range(0, 2):
        off_lines(0, j)
    for j in range(0, 2):
        off_lines(1, j)
    for j in range(0, 2):
        off_lines(2, j)
    for j in range(0, 2):
        off_lines(3, j)
    on_lines(0, 3)
    on_lines(1, 3)
    on_lines(2, 3)
    on_lines(3, 3)
    send_near(3)
    send_far(3)
    metas()
    for j in range(2, 4):
        off_lines(0, j)
    tail_keys()
    for j in range(2, 4):
        off_lines(1, j)
    choose(0)
    attend(0)
    give_back(0)
    for j in range(2, 4):
        off_lines(2, j)
    choose(1)
    attend(1)
    give_back(1)
    for j in range(2, 4):
        off_lines(3, j)
    choose(2)
    attend(2)
    give_back(2)
    choose(3)
    attend(3)
    give_back(3)

    for g in range(pairs):
        x_all(g).wait_send()
    m_all().wait_send()
    for g in range(pairs):
        spread(z, g, finish)

    def relayed(t, c):
        for g in range(pairs):
            on_line(t, g, finish, False)
        return c

    lax.fori_loop(1, line, relayed, 0)

    def crossed(t, c):
        for g in range(pairs):
            off_line(t, g, finish, False)
        return c

    if across > 1:
        lax.fori_loop(0, line, crossed, 0)

    for p in range(pairs):
        r_all(p).wait_recv()
        own_r(p).wait()
        for r in range(0, count, some):
            for i in range(some):
                flat[i * two : (i + 1) * two] = orx[p][slot_of[r + i]].astype(jnp.float32)
            for h in range(two):
                at = (p * two + h) * HD
                out_ref[r : r + some, at : at + HD] = flat[
                    pl.ds(h, some, stride=two), :
                ].astype(jnp.bfloat16)
    for p in range(pairs):
        r_all(p).wait_send()


def body(
    across, prompt_k, prompt_v, prompt_mask, shared_kv, shared_len, send_pick,
    unique_q, unique_kv, unique_owner,
):
    n = lax.axis_size("branch")
    rows = unique_q.shape[0]
    cap = 2 * rows // n
    width = n * cap
    res, rlen = shared_kv.shape[:2]
    heads = unique_q.shape[1] // HD
    kvh = unique_kv.shape[1] // (2 * HD)
    pairs = kvh // 2
    plen = prompt_k.shape[1]
    tail_n = -(-(n * rlen + width) // 128) * 128
    qrows = width * GRP
    hbm = pl.BlockSpec(memory_space=pltpu.HBM)
    bf, f32, i32 = jnp.bfloat16, jnp.float32, jnp.int32
    dma = pltpu.SemaphoreType.DMA
    buffers = [
        (unique_q.shape, bf),
        (unique_kv.shape, bf),
        (prompt_k.shape[1:], bf),
        (prompt_v.shape[1:], bf),
        ((max(min(rows, 16) * (heads + 2 * kvh), width * 2 * kvh), HD), f32),
        ((rows, heads + 2 * kvh, HD), bf),
        None,
        ((1, plen), f32),
        ((1, tail_n), f32),
        ((n, 1, HD), i32),
        ((width, heads + 2 * kvh, HD), bf),
        ((width, heads + 2 * kvh, HD), bf),
        ((n, 1, HD), i32),
        ((pairs, tail_n, 4 * HD), bf),
        ((1, tail_n), i32),
        ((width, heads, HD), bf),
    ]
    groups = [((width, 2 * GRP, HD), bf)] * pairs + [((n, res, rlen, 4 * HD), bf)] * pairs
    held = sum(
        math.prod(b[0]) * jnp.dtype(b[1]).itemsize for b in buffers + groups if b is not None
    )
    held += 2 * qrows * (plen + tail_n) * 4
    limit = min(67043328, held * 5 // 4 + 2 * rows * heads * HD + (4 << 20))
    out = pl.pallas_call(
        functools.partial(kernel, n, across, cap, rlen, res, heads),
        out_shape=jax.ShapeDtypeStruct((rows, heads * HD), bf),
        in_specs=[hbm] * 9,
        out_specs=pl.BlockSpec(memory_space=pltpu.VMEM),
        scratch_shapes=[
            pltpu.SMEM((rows,), i32),
            pltpu.SMEM(send_pick.shape, i32),
            pltpu.SMEM(shared_len.shape, i32),
            pltpu.SMEM(prompt_mask.shape, i32),
            pltpu.SMEM((n, 1, HD), i32),
            *[pltpu.SMEM((rows,), i32) if b is None else pltpu.VMEM(*b) for b in buffers],
            dma((9 + pairs,)),
            dma((pairs + 3,)),
            dma((1,)),
            dma((pairs,)),
            dma((1,)),
            dma((1,)),
            dma((1,)),
            dma((n // 2 * pairs,)),
            dma((pairs,)),
            dma((1,)),
            dma((pairs,)),
            *[pltpu.VMEM(*b) for b in groups],
        ],
        compiler_params=pltpu.CompilerParams(
            collective_id=0, has_side_effects=True, vmem_limit_bytes=limit
        ),
    )(
        *[
            pltpu.with_memory_space_constraint(v, pltpu.HBM)
            for v in (
                unique_owner.reshape(rows), send_pick, shared_len, prompt_mask,
                unique_q, unique_kv, shared_kv, prompt_k, prompt_v,
            )
        ]
    )
    return out


def chips_across(mesh):
    devices = mesh.devices.reshape(-1, mesh.shape["branch"])[0]
    try:
        places = [tuple(d.coords) for d in devices[::2]]
    except (AttributeError, TypeError):
        return 1
    return sum(1 for p in places if p[2] == places[0][2])


def solution(mesh):
    spec1, spec2, spec3 = (P(("groups", "branch"), *(None,) * k) for k in range(3))
    in_specs = (spec3, spec3, spec2, spec3, spec1, spec2, spec2, spec2, spec2)
    return jax.shard_map(
        functools.partial(body, chips_across(mesh)),
        mesh=mesh, in_specs=in_specs, out_specs=spec2, check_vma=False,
    )
```

time: 51.8 us -> 43.7 us (0.84)
  Pallas kernels: 49.9 us -> 42.8 us
  local copies, waits for them, and re-layouts: 1.67 us -> 0.71 us
    pallas_call x1, Pallas kernels: 49.9 us -> 42.8 us  [body(): pl.pallas_call(functools.partial(kernel, n, across, cap, rlen, res, heads...]
    unnamed x1, local copies, waits for them, and re-layouts: 1.67 us -> 0.71 us
where the time goes in v2:
time: 43.7 us; the launch traced here: 43.5 us
  Pallas kernels  42.8 us (98%)
  local copies, waits for them, and re-layouts  0.71 us (2%)
    pallas_call x1, Pallas kernels, body(): pl.pallas_call(functools.partial(kernel, n, across, cap, rlen, res, heads...  42.8 us

profile of v2, /device:TPU:0, one launch (start us, length us, event | category | flops | bytes accessed | tf_op | source)
XLA Modules:
  0.0 43.5 jit_solution(11736641040365276927)
XLA Ops:
  0.0 42.8 %shard_map.91 = bf16[16,8192]{1,0:T(8,128)(2,1)S(1)} custom-call(s32[16]{0:T(128)} %bitcast.1, s32[1,16]{1,0:T(1,128)} %pick_hbm.1, s32[2]{0:T(128)} %len_hbm.1, s32[1,8]{1,0:T(1,128)} %mask_hbm.1, bf16[16,8192]{1,0:T(8,128)(2,1)} %q_hbm.1, bf16[16,2048]{1,0:T(8,128)(2,1)} %kv_hbm.1, bf16[2,24,2048]{2,1,0:T(8,128)(2,1)} %shared_hbm.1, ...), custom_call_target="tpu_custom_call" | custom-call | tf_op jit(solution)/shard_map/pallas_call | solution.py:572
  42.8 0.7 %copy.11 = bf16[16,8192]{1,0:T(8,128)(2,1)} copy(bf16[16,8192]{1,0:T(8,128)(2,1)S(1)} %shard_map.91) | data formatting | bytes 524288

commit v3 on v2

--- a/solution.py
+++ b/solution.py
@@ -19,13 +19,13 @@
     owner_hbm, pick_hbm, len_hbm, mask_hbm, q_hbm, kv_hbm, shared_hbm, pk_hbm, pv_hbm,
     out_ref,
     owner_ref, pick_ref, len_ref, mask_ref, meta_in,
-    q_ref, kv_ref, pk, pv, flat, by_row, slot_of, pbias, tbias, meta_ref, xs, xr, mr, tail, kslot,
-    ox, lsem, osem, xsend, xrecv, msend, mrecv, gsend, grecv, srecv, rsend, rrecv, *by_group,
+    q_ref, kv_ref, pk, pv, flat, by_row, slot_of, pbias, tbias, meta_ref, mr, tail, kslot,
+    lsem, osem, xsend, xrecv, msend, mrecv, gsend, grecv, srecv, rsend, rrecv, rown, *by_group,
 ):
     me = lax.axis_index("branch")
     kvh = heads // GRP
     pairs = kvh // 2
-    orx, gath = by_group[:pairs], by_group[pairs:]
+    orx, ox, gath, xs, xr = (by_group[i * pairs : (i + 1) * pairs] for i in range(5))
     width = n * cap
     rows = width * GRP
     kvw = kvh * HD
@@ -54,7 +54,7 @@
         return pltpu.make_async_copy(
             shared_hbm.at[:, :, pl.ds(part * kvw + g * gw, gw)],
             gath[g].at[me, :, :, pl.ds(part * gw, gw)],
-            lsem.at[9 + g],
+            lsem.at[8 + g],
         )
 
     copy_q = pltpu.make_async_copy(q_hbm, q_ref, lsem.at[4])
@@ -160,14 +160,9 @@
         if across > 1:
             lax.fori_loop(cuts[j], cuts[j + 1], one, 0)
 
-    def group(g):
-        lo = 0 if g == 0 else g * two + 2 * kvh
-        return slice(lo, (g + 1) * two + 2 * kvh)
-
     def x_copy(g, b, at):
         return pltpu.make_async_remote_copy(
-            src_ref=xs.at[pl.ds(b * cap, cap), group(g)],
-            dst_ref=xr.at[pl.ds(at * cap, cap), group(g)],
+            src_ref=xs[g].at[pl.ds(b * cap, cap)], dst_ref=xr[g].at[pl.ds(at * cap, cap)],
             send_sem=xsend.at[0], recv_sem=xrecv.at[g],
             device_id={"branch": b}, device_id_type=MESH,
         )
@@ -179,31 +174,40 @@
             device_id={"branch": b}, device_id_type=MESH,
         )
 
-    def send_to(g, b):
-        x_copy(g, b, me).start()
-        if g == 0:
-            m_copy(b, me).start()
-
-    def send_x(g, d):
+    def each(columns, act):
         def one(i, c):
-            at = lax.rem(2 * z + core + i, 2 * line)
-            send_to(g, member(at // 2, lax.rem(y + d, across), lax.rem(at, 2)))
+            for up in (0, 1):
+                far = line - 1 - i
+                zt = z - far if up == 0 else z + far
+
+                @pl.when(zt >= 0 if up == 0 else zt < line)
+                def _():
+                    for d in columns:
+                        for cc in range(2):
+                            act(member(lax.rem(zt + line, line), lax.rem(y + d, across), cc))
+
             return c
 
-        lax.fori_loop(0 if d else 1, 2 * line, one, 0)
-
-    def send_near(g):
-        send_x(g, 0)
-
-    def send_far(g):
-        for d in range(1, across):
-            send_x(g, d)
+        lax.fori_loop(0, line - 1, one, 0)
+        for d in columns:
+            for cc in range(2) if d else ():
+                act(member(z, lax.rem(y + d, across), cc))
+        if 0 in columns:
+            act(sibling)
+
+    def send_x(g, columns):
+        def to(b):
+            x_copy(g, b, me).start()
+            if g == 0:
+                m_copy(b, me).start()
+
+        each(columns, to)
 
     others = pl.ds(0, (n - 1) * cap)
 
     def x_all(g):
         return pltpu.make_async_remote_copy(
-            src_ref=xs.at[others, group(g)], dst_ref=xr.at[others, group(g)],
+            src_ref=xs[g].at[others], dst_ref=xr[g].at[others],
             send_sem=xsend.at[0], recv_sem=xrecv.at[g],
             device_id={"branch": sibling}, device_id_type=MESH,
         )
@@ -224,14 +228,17 @@
 
     def loaded(g):
         mine = gath[g].at[me]
-        pltpu.make_async_copy(mine, mine, lsem.at[9 + g]).wait()
+        pltpu.make_async_copy(mine, mine, lsem.at[8 + g]).wait()
 
     loaded(0)
     pl.semaphore_wait(barrier, n - 1)
     own(0)
-    for g in range(1, pairs):
-        loaded(g)
-        own(g)
+    loaded(1)
+    own(1)
+    loaded(2)
+    own(2)
+    loaded(3)
+    own(3)
     for copy in small:
         copy.wait()
     count = q_ref.shape[0]
@@ -284,7 +291,9 @@
             lane == 0, pick, jnp.where(lane == 1, length, jnp.where(found[cap] > lane - 2, 1, 0))
         )
         for k in range(cap):
-            xs[b * cap + k] = by_row[found[k]]
+            for g in range(pairs):
+                lo = g * two + 2 * kvh if g else 0
+                xs[g][b * cap + k] = by_row[found[k], lo : (g + 1) * two + 2 * kvh]
         return c
 
     lax.fori_loop(0, n, place, 0)
@@ -298,12 +307,13 @@
     def part(ref, b):
         return ref.at[pl.ds(b * cap, cap)]
 
-    own_x = pltpu.make_async_copy(part(xs, me), part(xr, me), osem.at[pairs])
-    own_m = pltpu.make_async_copy(meta_ref.at[me], mr.at[me], osem.at[pairs + 1])
+    own_x = [
+        pltpu.make_async_copy(part(xs[g], me), part(xr[g], me), osem.at[g]) for g in range(pairs)
+    ]
+    own_m = pltpu.make_async_copy(meta_ref.at[me], mr.at[me], osem.at[pairs])
 
     def queries(p):
-        lo = 0 if p == 0 else p * two + 2 * kvh
-        both = xr[:, lo : lo + two, :].astype(jnp.float32)
+        both = xr[p][:, :two, :].astype(jnp.float32)
         return [
             both[:, k * GRP : (k + 1) * GRP].reshape(rows, HD).astype(jnp.bfloat16)
             for k in range(2)
@@ -312,7 +322,7 @@
     def scores(q, k):
         return lax.dot_general(q, k, (((1,), (1,)), ((), ())), preferred_element_type=jnp.float32)
 
-    copy_m = pltpu.make_async_copy(mr, meta_in, osem.at[pairs + 2])
+    copy_m = pltpu.make_async_copy(mr, meta_in, osem.at[pairs + 1])
 
     def metas():
         m_all().wait_recv()
@@ -342,10 +352,10 @@
         tbias[...] = jnp.where(shared_ok, 0.0, NEG)
         kslot[...] = jnp.where(shared_ok, -1, jnp.where(live > 0, col - n * rlen, width))
         x_all(0).wait_recv()
-        own_x.wait()
+        own_x[0].wait()
         kv_at = slice(two, two + 2 * kvh)
         flat[: width * 2 * kvh] = (
-            xr[:, kv_at, :].astype(jnp.float32).reshape(width * 2 * kvh, HD)
+            xr[0][:, kv_at, :].astype(jnp.float32).reshape(width * 2 * kvh, HD)
         )
         for j in range(2 * kvh):
             at = j % 2 + 2 * (j // kvh)
@@ -380,6 +390,7 @@
             copy_v.wait()
         else:
             x_all(p).wait_recv()
+            own_x[p].wait()
         done = []
         for k, q in enumerate(queries(p)):
             h = 2 * p + k
@@ -403,40 +414,33 @@
                 wp.astype(jnp.bfloat16), pv[:, cols], preferred_element_type=jnp.float32
             ) + jnp.dot(wt.astype(jnp.bfloat16), values, preferred_element_type=jnp.float32)
             done.append((mixed / total).reshape(width, GRP, HD))
-        ox[:, p * two : (p + 1) * two, :] = jnp.concatenate(done, axis=1).astype(jnp.bfloat16)
+        ox[p][...] = jnp.concatenate(done, axis=1).astype(jnp.bfloat16)
 
     def r_copy(p, b, at):
-        cut = slice(p * two, (p + 1) * two)
-        return pltpu.make_async_remote_copy(
-            src_ref=ox.at[pl.ds(b * cap, cap), cut], dst_ref=orx[p].at[pl.ds(at * cap, cap)],
+        return pltpu.make_async_remote_copy(
+            src_ref=ox[p].at[pl.ds(b * cap, cap)], dst_ref=orx[p].at[pl.ds(at * cap, cap)],
             send_sem=rsend.at[0], recv_sem=rrecv.at[p],
             device_id={"branch": b}, device_id_type=MESH,
         )
 
     def r_all(p):
-        cut = slice(p * two, (p + 1) * two)
-        return pltpu.make_async_remote_copy(
-            src_ref=ox.at[others, cut], dst_ref=orx[p].at[others],
+        return pltpu.make_async_remote_copy(
+            src_ref=ox[p].at[others], dst_ref=orx[p].at[others],
             send_sem=rsend.at[0], recv_sem=rrecv.at[p],
             device_id={"branch": sibling}, device_id_type=MESH,
         )
 
     def own_r(p):
-        cut = slice(p * two, (p + 1) * two)
-        return pltpu.make_async_copy(
-            ox.at[pl.ds(me * cap, cap), cut], orx[p].at[pl.ds(me * cap, cap)], osem.at[p]
-        )
+        return pltpu.make_async_copy(part(ox[p], me), part(orx[p], me), rown.at[p])
 
     def give_back(p):
-        def one(i, c):
-            r_copy(p, lax.rem(me + i, n), me).start()
-            return c
-
-        lax.fori_loop(1, n, one, 0)
+        each(range(across), lambda b: r_copy(p, b, me).start())
         own_r(p).start()
 
-    own_x.start()
+    for copy in own_x:
+        copy.start()
     own_m.start()
+    send_x(0, range(across))
     on_lines(0, 1)
     on_lines(1, 1)
     on_lines(2, 1)
@@ -444,16 +448,11 @@
     used = n * rlen + width
     if used < tail_n:
         tail[:, used:, :] = jnp.zeros((pairs, tail_n - used, 4 * HD), jnp.bfloat16)
-    send_near(0)
-    send_far(0)
     on_lines(0, 2)
     on_lines(1, 2)
+    send_x(1, range(across))
     on_lines(2, 2)
     on_lines(3, 2)
-    send_near(1)
-    send_far(1)
-    send_near(2)
-    send_far(2)
     for j in range(0, 2):
         off_lines(0, j)
     for j in range(0, 2):
@@ -463,11 +462,11 @@
     for j in range(0, 2):
         off_lines(3, j)
     on_lines(0, 3)
+    send_x(2, range(across))
     on_lines(1, 3)
     on_lines(2, 3)
     on_lines(3, 3)
-    send_near(3)
-    send_far(3)
+    send_x(3, range(across))
     metas()
     for j in range(2, 4):
         off_lines(0, j)
@@ -556,14 +555,13 @@
         ((1, plen), f32),
         ((1, tail_n), f32),
         ((n, 1, HD), i32),
-        ((width, heads + 2 * kvh, HD), bf),
-        ((width, heads + 2 * kvh, HD), bf),
         ((n, 1, HD), i32),
         ((pairs, tail_n, 4 * HD), bf),
         ((1, tail_n), i32),
-        ((width, heads, HD), bf),
     ]
-    groups = [((width, 2 * GRP, HD), bf)] * pairs + [((n, res, rlen, 4 * HD), bf)] * pairs
+    groups = [((width, 2 * GRP, HD), bf)] * (2 * pairs) + [((n, res, rlen, 4 * HD), bf)] * pairs
+    halves = [((width, 2 * GRP + (0 if g else 2 * kvh), HD), bf) for g in range(pairs)]
+    groups += halves * 2
     held = sum(
         math.prod(b[0]) * jnp.dtype(b[1]).itemsize for b in buffers + groups if b is not None
     )
@@ -581,8 +579,8 @@
             pltpu.SMEM(prompt_mask.shape, i32),
             pltpu.SMEM((n, 1, HD), i32),
             *[pltpu.SMEM((rows,), i32) if b is None else pltpu.VMEM(*b) for b in buffers],
-            dma((9 + pairs,)),
-            dma((pairs + 3,)),
+            dma((8 + pairs,)),
+            dma((pairs + 2,)),
             dma((1,)),
             dma((pairs,)),
             dma((1,)),
@@ -591,6 +589,7 @@
             dma((n // 2 * pairs,)),
             dma((pairs,)),
             dma((1,)),
+            dma((pairs,)),
             dma((pairs,)),
             *[pltpu.VMEM(*b) for b in groups],
         ],

time: 43.7 us -> 43.4 us (level)
  no operation moved by 1% of the time
where the time goes in v3:
time: 43.4 us; the launch traced here: 43.2 us
  Pallas kernels  42.5 us (98%)
  local copies, waits for them, and re-layouts  0.71 us (2%)
    pallas_call x1, Pallas kernels, body(): pl.pallas_call(functools.partial(kernel, n, across, cap, rlen, res, heads...  42.5 us

profile of v3, /device:TPU:0, one launch (start us, length us, event | category | flops | bytes accessed | tf_op | source)
XLA Modules:
  0.0 43.2 jit_solution(15038315394841946283)
XLA Ops:
  0.0 42.5 %shard_map.91 = bf16[16,8192]{1,0:T(8,128)(2,1)S(1)} custom-call(s32[16]{0:T(128)} %bitcast.1, s32[1,16]{1,0:T(1,128)} %pick_hbm.1, s32[2]{0:T(128)} %len_hbm.1, s32[1,8]{1,0:T(1,128)} %mask_hbm.1, bf16[16,8192]{1,0:T(8,128)(2,1)} %q_hbm.1, bf16[16,2048]{1,0:T(8,128)(2,1)} %kv_hbm.1, bf16[2,24,2048]{2,1,0:T(8,128)(2,1)} %shared_hbm.1, ...), custom_call_target="tpu_custom_call" | custom-call | tf_op jit(solution)/shard_map/pallas_call | solution.py:570
  42.5 0.7 %copy.11 = bf16[16,8192]{1,0:T(8,128)(2,1)} copy(bf16[16,8192]{1,0:T(8,128)(2,1)S(1)} %shard_map.91) | data formatting | bytes 524288

commit v4 on v3

--- a/solution.py
+++ b/solution.py
@@ -20,7 +20,7 @@
     out_ref,
     owner_ref, pick_ref, len_ref, mask_ref, meta_in,
     q_ref, kv_ref, pk, pv, flat, by_row, slot_of, pbias, tbias, meta_ref, mr, tail, kslot,
-    lsem, osem, xsend, xrecv, msend, mrecv, gsend, grecv, srecv, rsend, rrecv, rown, *by_group,
+    lsem, osem, xsend, xrecv, msend, mrecv, gsend, grecv, srecv, rsend, rrecv, *by_group,
 ):
     me = lax.axis_index("branch")
     kvh = heads // GRP
@@ -304,14 +304,6 @@
             (1, block), jnp.where(mask_ref[0, g] > 0, 0.0, NEG), jnp.float32
         )
 
-    def part(ref, b):
-        return ref.at[pl.ds(b * cap, cap)]
-
-    own_x = [
-        pltpu.make_async_copy(part(xs[g], me), part(xr[g], me), osem.at[g]) for g in range(pairs)
-    ]
-    own_m = pltpu.make_async_copy(meta_ref.at[me], mr.at[me], osem.at[pairs])
-
     def queries(p):
         both = xr[p][:, :two, :].astype(jnp.float32)
         return [
@@ -322,11 +314,10 @@
     def scores(q, k):
         return lax.dot_general(q, k, (((1,), (1,)), ((), ())), preferred_element_type=jnp.float32)
 
-    copy_m = pltpu.make_async_copy(mr, meta_in, osem.at[pairs + 1])
+    copy_m = pltpu.make_async_copy(mr, meta_in, osem.at[0])
 
     def metas():
         m_all().wait_recv()
-        own_m.wait()
         copy_m.start()
 
     def tail_keys():
@@ -352,7 +343,6 @@
         tbias[...] = jnp.where(shared_ok, 0.0, NEG)
         kslot[...] = jnp.where(shared_ok, -1, jnp.where(live > 0, col - n * rlen, width))
         x_all(0).wait_recv()
-        own_x[0].wait()
         kv_at = slice(two, two + 2 * kvh)
         flat[: width * 2 * kvh] = (
             xr[0][:, kv_at, :].astype(jnp.float32).reshape(width * 2 * kvh, HD)
@@ -390,7 +380,6 @@
             copy_v.wait()
         else:
             x_all(p).wait_recv()
-            own_x[p].wait()
         done = []
         for k, q in enumerate(queries(p)):
             h = 2 * p + k
@@ -430,16 +419,14 @@
             device_id={"branch": sibling}, device_id_type=MESH,
         )
 
-    def own_r(p):
-        return pltpu.make_async_copy(part(ox[p], me), part(orx[p], me), rown.at[p])
-
     def give_back(p):
         each(range(across), lambda b: r_copy(p, b, me).start())
-        own_r(p).start()
-
-    for copy in own_x:
-        copy.start()
-    own_m.start()
+        orx[p][mine] = ox[p][mine]
+
+    mine = pl.ds(me * cap, cap)
+    for g in range(pairs):
+        xr[g][mine] = xs[g][mine]
+    mr[me] = meta_ref[me]
     send_x(0, range(across))
     on_lines(0, 1)
     on_lines(1, 1)
@@ -513,7 +500,6 @@
 
     for p in range(pairs):
         r_all(p).wait_recv()
-        own_r(p).wait()
         for r in range(0, count, some):
             for i in range(some):
                 flat[i * two : (i + 1) * two] = orx[p][slot_of[r + i]].astype(jnp.float32)
@@ -580,7 +566,7 @@
             pltpu.SMEM((n, 1, HD), i32),
             *[pltpu.SMEM((rows,), i32) if b is None else pltpu.VMEM(*b) for b in buffers],
             dma((8 + pairs,)),
-            dma((pairs + 2,)),
+            dma((1,)),
             dma((1,)),
             dma((pairs,)),
             dma((1,)),
@@ -589,7 +575,6 @@
             dma((n // 2 * pairs,)),
             dma((pairs,)),
             dma((1,)),
-            dma((pairs,)),
             dma((pairs,)),
             *[pltpu.VMEM(*b) for b in groups],
         ],

time: 43.4 us -> 43.4 us (level)
  no operation moved by 1% of the time
where the time goes in v4:
time: 43.4 us; the launch traced here: 43.1 us
  Pallas kernels  42.4 us (98%)
  local copies, waits for them, and re-layouts  0.71 us (2%)
    pallas_call x1, Pallas kernels, body(): pl.pallas_call(functools.partial(kernel, n, across, cap, rlen, res, heads...  42.4 us

profile of v4, /device:TPU:0, one launch (start us, length us, event | category | flops | bytes accessed | tf_op | source)
XLA Modules:
  0.0 43.1 jit_solution(2379499875819746131)
XLA Ops:
  0.0 42.4 %shard_map.91 = bf16[16,8192]{1,0:T(8,128)(2,1)S(1)} custom-call(s32[16]{0:T(128)} %bitcast.1, s32[1,16]{1,0:T(1,128)} %pick_hbm.1, s32[2]{0:T(128)} %len_hbm.1, s32[1,8]{1,0:T(1,128)} %mask_hbm.1, bf16[16,8192]{1,0:T(8,128)(2,1)} %q_hbm.1, bf16[16,2048]{1,0:T(8,128)(2,1)} %kv_hbm.1, bf16[2,24,2048]{2,1,0:T(8,128)(2,1)} %shared_hbm.1, ...), custom_call_target="tpu_custom_call" | custom-call | tf_op jit(solution)/shard_map/pallas_call | solution.py:556
  42.4 0.7 %copy.11 = bf16[16,8192]{1,0:T(8,128)(2,1)} copy(bf16[16,8192]{1,0:T(8,128)(2,1)S(1)} %shard_map.91) | data formatting | bytes 524288
